TPU v7x, 32 devices: a whole 2x2x4 slice. The times are simulated.
32 devices in a mesh: shard: 4 (over z), ctx: 4 (over x, core), tp: 2 (over y).
Axes of the slice: x: 2, y: 2, z: 4, core: 2. Of those that a mesh axis runs over, the one named last changes fastest.
Arguments:
- inputs: bfloat16 [4, 2048, 2048], P('shard', 'ctx'), may hold values from -6 to 6
- cotangent: bfloat16 [4, 2048, 2048], P('shard', 'ctx'), may hold values from -6 to 6
- query_weight: bfloat16 [2048, 2048], P('shard', 'tp'), may hold values from -0.1875 to 0.1875
- key_weight: bfloat16 [2048, 2048], P('shard', 'tp'), may hold values from -0.1875 to 0.1875
- value_weight: bfloat16 [2048, 2048], P('shard', 'tp'), may hold values from -0.125 to 0.125
- output_weight: bfloat16 [2048, 2048], P('shard', 'tp'), may hold values from -0.75 to 0.75
- up_weight: bfloat16 [2048, 8192], P('shard', 'tp'), may hold values from -0.125 to 0.125
- down_weight: bfloat16 [2048, 8192], P('shard', 'tp'), may hold values from -0.0625 to 0.0625
- query_value_bias: bfloat16 [2, 16, 128], P(None, 'tp', 'shard'), may hold values from -3 to 3
- up_bias: bfloat16 [64, 128], P('tp', 'shard'), may hold values from -3 to 3
- norm_gains: bfloat16 [2, 16, 128], P(None, 'tp', 'shard'), may hold values from 0.25 to 1.75
- other_biases: bfloat16 [4, 16, 128], P(None, 'tp', 'shard'), may hold values from -2 to 2
Outputs:
- outputs: bfloat16 [4, 2048, 2048], P('shard', 'ctx')
- input_grad: bfloat16 [4, 2048, 2048], P('shard', 'ctx')
- grad_query: float32 [2048, 2048], P('shard', 'tp')
- grad_key: float32 [2048, 2048], P('shard', 'tp')
- grad_value: float32 [2048, 2048], P('shard', 'tp')
- grad_output: float32 [2048, 2048], P('shard', 'tp')
- grad_up: float32 [2048, 8192], P('shard', 'tp')
- grad_down: float32 [2048, 8192], P('shard', 'tp')
- grad_qv_bias: float32 [2, 16, 128], P(None, 'tp', 'shard')
- grad_up_bias: float32 [64, 128], P('tp', 'shard')
- grad_gains: float32 [2, 16, 128], P(None, 'tp', 'shard')
- grad_biases: float32 [4, 16, 128], P(None, 'tp', 'shard')
- root_squares: float32 [3], replicated
All inputs are finite; a program needn't handle non-finite values.
Results may differ from a plain program's by a relative error of at most 0.024.
Values may be sent and summed in bfloat16 or wider, within the bound.
No kernel may reach another device: no remote copies, remote signals or barrier semaphores. Data moves between devices by JAX's collectives and lax.ppermute only.
A program may use at most 320 MiB of HBM per device.

v0:
```python
import jax
import jax.numpy as jnp
from jax import lax
from jax.sharding import PartitionSpec as P

D = 2048
H = 16
DH = 128
epsilon = 1e-12


def product(left, right):
    return jnp.dot(left, right, preferred_element_type=jnp.float32)


def times_transposed(left, right):
    return lax.dot_general(
        left, right, (((1,), (1,)), ((), ())), preferred_element_type=jnp.float32
    )


def transposed_times(left, right):
    return lax.dot_general(
        left, right, (((0,), (0,)), ((), ())), preferred_element_type=jnp.float32
    )


def normalize(stream):
    center = stream - jnp.mean(stream, axis=-1, keepdims=True)
    factor = lax.rsqrt(jnp.mean(center * center, axis=-1, keepdims=True) + epsilon)
    return (center * factor, factor)


def norm_backward(grad_norm, normed, factor):
    return factor * (
        grad_norm
        - jnp.mean(grad_norm, axis=-1, keepdims=True)
        - normed * jnp.mean(grad_norm * normed, axis=-1, keepdims=True)
    )


def gelu_tanh(values):
    return jax.nn.gelu(values, approximate=True)


def split_heads(matrix, heads_here):
    return matrix.reshape(matrix.shape[0], heads_here, DH).transpose(1, 0, 2)


def merge_heads(stacked):
    return stacked.transpose(1, 0, 2).reshape(stacked.shape[1], stacked.shape[0] * stacked.shape[2])


def head_forward(triple):
    q_head, k_head, v_head = triple
    scores = times_transposed(q_head, k_head) * DH ** (-0.5)
    peak = jnp.max(scores, axis=-1, keepdims=True)
    expo = jnp.exp(scores - peak)
    total = jnp.sum(expo, axis=-1, keepdims=True)
    probs = expo / total
    result = product(probs.astype(jnp.bfloat16), v_head)
    return (result, (peak + jnp.log(total))[:, 0])


def head_backward(group):
    q_head, k_head, v_head, d_head, logsum = group
    scale = DH ** (-0.5)
    scores = times_transposed(q_head, k_head) * scale
    probs = jnp.exp(scores - logsum[:, None])
    d_probs = times_transposed(d_head, v_head)
    inner = jnp.sum(probs * d_probs, axis=-1, keepdims=True)
    d_scores = (probs * (d_probs - inner)).astype(jnp.bfloat16)
    d_query = product(d_scores, k_head) * scale
    d_key = transposed_times(d_scores, q_head) * scale
    d_value = transposed_times(probs.astype(jnp.bfloat16), d_head)
    return (d_query, d_key, d_value)


def shards(
    inputs,
    cotangent,
    query_weight,
    key_weight,
    value_weight,
    output_weight,
    up_weight,
    down_weight,
    query_value_bias,
    up_bias,
    norm_gains,
    other_biases,
):
    local_rows = inputs.shape[1]
    tokens = inputs.reshape(local_rows, D)
    grad_out = cotangent.reshape(local_rows, D).astype(jnp.float32)
    gathered = (
        lax.all_gather(query_weight, "shard", axis=0, tiled=True),
        lax.all_gather(key_weight, "shard", axis=0, tiled=True),
        lax.all_gather(value_weight, "shard", axis=0, tiled=True),
        lax.all_gather(output_weight, "shard", axis=0, tiled=True),
        lax.all_gather(query_value_bias, "shard", axis=2, tiled=True),
        lax.all_gather(norm_gains, "shard", axis=2, tiled=True),
        lax.all_gather(other_biases, "shard", axis=2, tiled=True),
    )
    query_full, key_full, value_full, output_full, qv_full, gain_half, bias_half = gathered
    gain_whole, bias_whole = (
        lax.all_gather(gain_half, "tp", axis=1, tiled=True),
        lax.all_gather(bias_half, "tp", axis=1, tiled=True),
    )
    gains = gain_whole.reshape(2, D).astype(jnp.float32)
    biases = bias_whole.reshape(4, D).astype(jnp.float32)
    half_width = query_full.shape[1]
    heads_here = half_width // DH
    qv_vector = qv_full.reshape(2, half_width).astype(jnp.float32)
    queries = (product(tokens, query_full) + qv_vector[0]).astype(jnp.bfloat16)
    keys_mine = product(tokens, key_full).astype(jnp.bfloat16)
    values_mine = (product(tokens, value_full) + qv_vector[1]).astype(jnp.bfloat16)
    keys_all, values_all = (
        lax.all_gather(keys_mine, "ctx", axis=0, tiled=True),
        lax.all_gather(values_mine, "ctx", axis=0, tiled=True),
    )
    query_heads = split_heads(queries, heads_here)
    key_heads = split_heads(keys_all, heads_here)
    value_heads = split_heads(values_all, heads_here)
    head_out, logsums = lax.map(head_forward, (query_heads, key_heads, value_heads))
    attended = merge_heads(head_out).astype(jnp.bfloat16)
    attn_part = times_transposed(attended, output_full)
    attn_branch = lax.psum(attn_part.astype(jnp.bfloat16), "tp").astype(jnp.float32) + biases[0]
    normed_one, factor_one = normalize(tokens.astype(jnp.float32) + attn_branch)
    hidden_one = normed_one * gains[0] + biases[1]
    hidden_low = hidden_one.astype(jnp.bfloat16)
    up_full, down_full, up_bias_full = (
        lax.all_gather(up_weight, "shard", axis=0, tiled=True),
        lax.all_gather(down_weight, "shard", axis=0, tiled=True),
        lax.all_gather(up_bias, "shard", axis=1, tiled=True),
    )
    pre_act = product(hidden_low, up_full) + up_bias_full.reshape(-1).astype(jnp.float32)
    activated = gelu_tanh(pre_act).astype(jnp.bfloat16)
    mlp_part = times_transposed(activated, down_full)
    mlp_branch = lax.psum(mlp_part.astype(jnp.bfloat16), "tp").astype(jnp.float32) + biases[2]
    second = hidden_one + mlp_branch
    normed_two, factor_two = normalize(second)
    result = normed_two * gains[1] + biases[3]
    square_sums = jnp.stack(
        [
            jnp.sum(second * second),
            jnp.sum(attn_branch * attn_branch),
            jnp.sum(mlp_branch * mlp_branch),
        ]
    )
    grad_second = norm_backward(grad_out * gains[1], normed_two, factor_two)
    grad_mlp = grad_second.astype(jnp.bfloat16)
    grad_act = product(grad_mlp, down_full)
    unused, gelu_pull = jax.vjp(gelu_tanh, pre_act)
    grad_pre = gelu_pull(grad_act)[0].astype(jnp.bfloat16)
    hidden_part = times_transposed(grad_pre, up_full)
    grad_hidden = grad_second + lax.psum(hidden_part.astype(jnp.bfloat16), "tp").astype(jnp.float32)
    grad_first = norm_backward(grad_hidden * gains[0], normed_one, factor_one)
    grad_branch = grad_first.astype(jnp.bfloat16)
    grad_attended = product(grad_branch, output_full).astype(jnp.bfloat16)
    grad_heads = split_heads(grad_attended, heads_here)
    dq_heads, dk_heads, dv_heads = lax.map(
        head_backward, (query_heads, key_heads, value_heads, grad_heads, logsums)
    )
    grad_queries = merge_heads(dq_heads).astype(jnp.bfloat16)
    key_sums, value_sums = (
        lax.psum_scatter(
            merge_heads(dk_heads).astype(jnp.bfloat16), "ctx", scatter_dimension=0, tiled=True
        ).astype(jnp.float32),
        lax.psum_scatter(
            merge_heads(dv_heads).astype(jnp.bfloat16), "ctx", scatter_dimension=0, tiled=True
        ).astype(jnp.float32),
    )
    grad_keys = key_sums.astype(jnp.bfloat16)
    grad_values = value_sums.astype(jnp.bfloat16)
    input_part = (
        times_transposed(grad_queries, query_full)
        + times_transposed(grad_keys, key_full)
        + times_transposed(grad_values, value_full)
    )
    input_grad = grad_first + lax.psum(input_part.astype(jnp.bfloat16), "tp").astype(jnp.float32)
    qv_sums = jnp.stack(
        [
            jnp.sum(grad_queries.astype(jnp.float32), axis=0),
            jnp.sum(grad_values.astype(jnp.float32), axis=0),
        ]
    )
    up_sums = jnp.sum(grad_pre.astype(jnp.float32), axis=0)
    gain_sums = jnp.stack(
        [jnp.sum(grad_hidden * normed_one, axis=0), jnp.sum(grad_out * normed_two, axis=0)]
    )
    bias_sums = jnp.stack(
        [
            jnp.sum(grad_branch.astype(jnp.float32), axis=0),
            jnp.sum(grad_hidden, axis=0),
            jnp.sum(grad_mlp.astype(jnp.float32), axis=0),
            jnp.sum(grad_out, axis=0),
        ]
    )
    qv_total, up_total, gain_total, bias_total, square_total = lax.psum(
        (qv_sums, up_sums, gain_sums, bias_sums, square_sums), ("shard", "ctx")
    )
    summed = lax.psum_scatter(
        jnp.concatenate(
            [
                transposed_times(tokens, grad_queries),
                transposed_times(tokens, grad_keys),
                transposed_times(tokens, grad_values),
                transposed_times(grad_branch, attended),
                transposed_times(hidden_low, grad_pre),
                transposed_times(grad_mlp, activated),
            ],
            axis=1,
        ).astype(jnp.bfloat16),
        "shard",
        scatter_dimension=0,
        tiled=True,
    ).astype(jnp.float32)
    summed = lax.psum(summed.astype(jnp.bfloat16), "ctx").astype(jnp.float32)
    ff_half = up_full.shape[1]
    grad_query = summed[:, 0:half_width]
    grad_key = summed[:, half_width : 2 * half_width]
    grad_value = summed[:, 2 * half_width : 3 * half_width]
    grad_output = summed[:, 3 * half_width : 4 * half_width]
    grad_up = summed[:, 4 * half_width : 4 * half_width + ff_half]
    grad_down = summed[:, 4 * half_width + ff_half : 4 * half_width + 2 * ff_half]
    shard_index = lax.axis_index("shard")
    tp_index = lax.axis_index("tp")
    piece = DH // lax.axis_size("shard")
    heads_part = H // lax.axis_size("tp")
    grad_qv_bias = lax.dynamic_slice_in_dim(
        qv_total.reshape(2, heads_here, DH), shard_index * piece, piece, 2
    )
    grad_up_bias = lax.dynamic_slice_in_dim(
        up_total.reshape(ff_half // DH, DH), shard_index * piece, piece, 1
    )
    gain_rows = lax.dynamic_slice_in_dim(
        gain_total.reshape(2, H, DH), tp_index * heads_part, heads_part, 1
    )
    grad_gains = lax.dynamic_slice_in_dim(gain_rows, shard_index * piece, piece, 2)
    bias_rows = lax.dynamic_slice_in_dim(
        bias_total.reshape(4, H, DH), tp_index * heads_part, heads_part, 1
    )
    grad_biases = lax.dynamic_slice_in_dim(bias_rows, shard_index * piece, piece, 2)
    count_all = local_rows * lax.axis_size("shard") * lax.axis_size("ctx") * D
    root_squares = jnp.sqrt(square_total / count_all)
    outputs = result.astype(jnp.bfloat16).reshape(1, local_rows, D)
    input_out = input_grad.astype(jnp.bfloat16).reshape(1, local_rows, D)
    return (
        outputs,
        input_out,
        grad_query,
        grad_key,
        grad_value,
        grad_output,
        grad_up,
        grad_down,
        grad_qv_bias,
        grad_up_bias,
        grad_gains,
        grad_biases,
        root_squares,
    )


def solution(mesh):
    placed = (
        P("shard", "ctx", None),
        P("shard", "ctx", None),
        P("shard", "tp"),
        P("shard", "tp"),
        P("shard", "tp"),
        P("shard", "tp"),
        P("shard", "tp"),
        P("shard", "tp"),
        P(None, "tp", "shard"),
        P("tp", "shard"),
        P(None, "tp", "shard"),
        P(None, "tp", "shard"),
    )
    return jax.shard_map(
        shards,
        mesh=mesh,
        in_specs=placed,
        out_specs=(
            P("shard", "ctx", None),
            P("shard", "ctx", None),
            P("shard", "tp"),
            P("shard", "tp"),
            P("shard", "tp"),
            P("shard", "tp"),
            P("shard", "tp"),
            P("shard", "tp"),
            P(None, "tp", "shard"),
            P("tp", "shard"),
            P(None, "tp", "shard"),
            P(None, "tp", "shard"),
            P(),
        ),
        check_vma=False,
    )
```

profile of v0, /device:TPU:0, one launch (start us, length us, event | category | flops | bytes accessed | tf_op | source)
XLA Modules:
  0.0 2774.8 jit_solution(6751861890759885194)
XLA Ops:
  9.5 83.6 %all-gather.11.cloned.1.call-done = bf16[2048,1024]{1,0:T(8,128)(2,1)} async-done(((bf16[512,1024]{1,0:T(8,128)(2,1)}), bf16[2048,1024]{1,0:T(8,128)(2,1)}) %all-gather.11.cloned.1.call-update) | async-done | bytes 4194320 | tf_op jit(solution)/shard_map/all_gather | solution.py:98
  99.4 13.9 all_gather.43
  113.3 61.1 %all-gather.15.cloned.1.call-done = bf16[2048,1024]{1,0:T(8,128)(2,1)} async-done(((bf16[512,1024]{1,0:T(8,128)(2,1)}), bf16[2048,1024]{1,0:T(8,128)(2,1)}) %all-gather.15.cloned.1.call-update) | async-done | bytes 4194320 | tf_op jit(solution)/shard_map/all_gather | solution.py:99
  181.1 74.2 %all-gather.9.cloned.1.call-done = bf16[2048,1024]{1,0:T(8,128)(2,1)} async-done(((bf16[512,1024]{1,0:T(8,128)(2,1)}), bf16[2048,1024]{1,0:T(8,128)(2,1)}) %all-gather.9.cloned.1.call-update) | async-done | bytes 4194320 | tf_op jit(solution)/shard_map/all_gather | solution.py:97
  260.0 30.2 %all-gather.13.cloned.1.call-done = bf16[2048,1024]{1,0:T(8,128)(2,1)} async-done(((bf16[512,1024]{1,0:T(8,128)(2,1)}), bf16[2048,1024]{1,0:T(8,128)(2,1)}) %all-gather.13.cloned.1.call-update) | async-done | bytes 4194320 | tf_op jit(solution)/shard_map/all_gather | solution.py:119
  295.2 31.5 %all-gather.17.cloned.1.call-done = bf16[2048,1024]{1,0:T(8,128)(2,1)} async-done(((bf16[512,1024]{1,0:T(8,128)(2,1)}), bf16[2048,1024]{1,0:T(8,128)(2,1)}) %all-gather.17.cloned.1.call-update) | async-done | bytes 4194320 | tf_op jit(solution)/shard_map/all_gather | solution.py:120
  332.7 44.9 %while.26 = (s32[]{:T(128)}, bf16[8,512,128]{1,2,0:T(8,128)(2,1)}, f32[8,512]{1,0:T(8,128)S(1)}, bf16[8,512,128]{2,1,0:T(8,128)(2,1)S(1)}, bf16[8,2048,128]{2,1,...) while((s32[]{:T(128)}, bf16[8,512,128]{1,2,0:T(8,128)(2,1)}, ...), condition=%wide.region_3.4_spmd, body=%wide.region_0.3_spmd.sunk | while | flops 546307584 | bytes 14047329 | solution.py:125
  377.6 31.3 %all-gather.19.cloned.1.call-done = bf16[2048,1024]{1,0:T(8,128)(2,1)} async-done(((bf16[512,1024]{1,0:T(8,128)(2,1)}), bf16[2048,1024]{1,0:T(8,128)(2,1)}) %all-gather.19.cloned.1.call-update) | async-done | bytes 4194320 | tf_op jit(solution)/shard_map/all_gather | solution.py:100
  480.6 284.8 %all-gather.21.cloned.1.call-done = bf16[2048,4096]{1,0:T(8,128)(2,1)} async-done(((bf16[512,4096]{1,0:T(8,128)(2,1)}), bf16[2048,4096]{1,0:T(8,128)(2,1)}) %all-gather.21.cloned.1.call-update) | async-done | bytes 16777232 | tf_op jit(solution)/shard_map/all_gather | solution.py:133
  765.3 15.4 fusion.81
  780.7 271.1 %all-gather.23.cloned.1.call-done = bf16[2048,4096]{1,0:T(8,128)(2,1)} async-done(((bf16[512,4096]{1,0:T(8,128)(2,1)}), bf16[2048,4096]{1,0:T(8,128)(2,1)}) %all-gather.23.cloned.1.call-update) | async-done | bytes 16777232 | tf_op jit(solution)/shard_map/all_gather | solution.py:134
  1051.9 17.6 convolution_convert_fusion.3
  1069.8 61.1 %all-reduce.10.cloned.1.call-done = bf16[512,2048]{1,0:T(8,128)(2,1)} async-done(((bf16[512,2048]{1,0:T(8,128)(2,1)}), bf16[512,2048]{1,0:T(8,128)(2,1)}) %all-reduce.10.cloned.1.call-update) | async-done | bytes 2097168 | tf_op jit(solution)/shard_map/psum | solution.py:140
  1143.2 20.5 convert_reduce_fusion
  1179.1 63.0 %all-reduce.12.cloned.1.call-done = bf16[512,2048]{1,0:T(8,128)(2,1)} async-done(((bf16[512,2048]{1,0:T(8,128)(2,1)}), bf16[512,2048]{1,0:T(8,128)(2,1)}) %all-reduce.12.cloned.1.call-update) | async-done | bytes 2097168 | tf_op jit(solution)/shard_map/psum | solution.py:157
  1258.9 138.9 %while.27 = (s32[]{:T(128)}, bf16[8,512,128]{1,2,0:T(8,128)(2,1)}, bf16[8,2048,128]{1,2,0:T(8,128)(2,1)}, bf16[8,2048,128]{1,2,0:T(8,128)(2,1)}, bf16[8,512,128]...) while((s32[]{:T(128)}, bf16[8,512,128]{1,2,0:T(8,128)(2,1)}, ...), condition=%wide.region_17.18_spmd, body=%wide.region_15.17_spmd.sunk | while | flops 1351220736 | bytes 71447792 | solution.py:162
  1427.9 14.5 reduce-scatter.4.cloned.1.call-done
  1454.7 34.8 %reduce-scatter.6.cloned.1.call-done = bf16[512,1024]{0,1:T(8,128)(2,1)} async-done(((bf16[2048,1024]{0,1:T(8,128)(2,1)}), bf16[512,1024]{0,1:T(8,128)(2,1)}) %reduce-scatter.6.cloned.1.call-update) | async-done | bytes 1048592 | tf_op jit(solution)/shard_map/reduce_scatter | solution.py:170
  1512.5 15.4 convert_dynamic-update-slice_fusion.1
  1527.9 16.3 convert_dynamic-update-slice_fusion
  1567.3 797.9 %reduce-scatter.8.cloned.1.call-done = bf16[512,12288]{1,0:T(8,128)(2,1)} async-done(((bf16[2048,12288]{1,0:T(8,128)(2,1)}), bf16[512,12288]{1,0:T(8,128)(2,1)}) %reduce-scatter.8.cloned.1.call-update) | async-done | bytes 12582928 | tf_op jit(solution)/shard_map/reduce_scatter | solution.py:203
  2365.3 95.1 %all-reduce.18.cloned.1.call-done = (f32[2,8,128]{2,1,0:T(8,128)}, f32[32,128]{1,0:T(8,128)}, f32[2,16,128]{2,1,0:T(8,128)}, f32[4,16,128]{2,1,0:T(8,128)}, f32[3]{0:T(128)}) async-done(((f32[2,8,128]{2,1,0:T(8,128)}, f32[32,128]{1,0:T(8,128)}, f32[2,16,128]{2,1,0:T(8,128)}, f32[4,16,128]{2,1,0:T(8,128)}, f32[3]{0:T(128)}), (f32[2,8,128]{2,1,0:T(8,128)}, f32[32,128]{1,0:T(8,128)}, f32[2,16,128]{2,1,0:T(8,128)}, ...) | async-done | bytes 73756 | tf_op jit(solution)/shard_map/psum | solution.py:200
  2467.2 60.1 %all-reduce.14.cloned.1.call-done = bf16[512,2048]{1,0:T(8,128)(2,1)} async-done(((bf16[512,2048]{1,0:T(8,128)(2,1)}), bf16[512,2048]{1,0:T(8,128)(2,1)}) %all-reduce.14.cloned.1.call-update) | async-done | bytes 2097168 | tf_op jit(solution)/shard_map/psum | solution.py:181
  2532.1 218.1 %all-reduce.16.cloned.1.call-done = bf16[512,12288]{1,0:T(8,128)(2,1)} async-done(((bf16[512,12288]{1,0:T(8,128)(2,1)}), bf16[512,12288]{1,0:T(8,128)(2,1)}) %all-reduce.16.cloned.1.call-update) | async-done | bytes 12582928 | tf_op jit(solution)/shard_map/psum | solution.py:219
  (374 shorter events, 447.9 us)
Async XLA Ops:
  7.2 85.9 %all-gather.11.cloned.1.call-start = ((), (), s32[]{:S(2)}) async-start(), calls=%async_computation.4 | async-start | bytes 5242880 | tf_op jit(solution)/shard_map/all_gather | solution.py:98
  7.9 166.5 %all-gather.15.cloned.1.call-start = ((), (), s32[]{:S(2)}) async-start(), calls=%async_computation.6 | async-start | bytes 5242880 | tf_op jit(solution)/shard_map/all_gather | solution.py:99
  8.7 246.6 %all-gather.9.cloned.1.call-start = ((), (), s32[]{:S(2)}) async-start(), calls=%async_computation.3 | async-start | bytes 5242880 | tf_op jit(solution)/shard_map/all_gather | solution.py:97
  9.4 89.9 %copy-start.30 = (bf16[2,8,32]{2,1,0:T(8,128)(2,1)S(1)}, bf16[2,8,32]{2,1,0:T(8,128)(2,1)}, u32[]{:S(2)}) copy-start(bf16[2,8,32]{2,1,0:T(8,128)(2,1)} %param.24) | copy-start | bytes 3076
  9.4 165.0 %copy-start.1 = (bf16[1,512,2048]{2,1,0:T(8,128)(2,1)S(1)}, bf16[1,512,2048]{2,1,0:T(8,128)(2,1)}, u32[]{:S(2)}) copy-start(bf16[1,512,2048]{2,1,0:T(8,128)(2,1)} %param.16) | copy-start | bytes 6291460
  9.4 280.8 %all-gather.13.cloned.1.call-start = ((), (), s32[]{:S(2)}) async-start(), calls=%async_computation.5 | async-start | bytes 5242880 | tf_op jit(solution)/shard_map/all_gather | solution.py:119
  99.2 227.5 %all-gather.17.cloned.1.call-start = ((), (), s32[]{:S(2)}) async-start(), calls=%async_computation.7 | async-start | bytes 5242880 | tf_op jit(solution)/shard_map/all_gather | solution.py:120
  180.0 229.0 %all-gather.19.cloned.1.call-start = ((), (), s32[]{:S(2)}) async-start(), calls=%async_computation.8 | async-start | bytes 5242880 | tf_op jit(solution)/shard_map/all_gather | solution.py:100
  180.5 296.4 %all-reduce.8.cloned.1.call-start = ((), (), s32[]{:S(2)}) async-start(), calls=%async_computation.9 | async-start | bytes 4194304 | tf_op jit(solution)/shard_map/psum | solution.py:128
  415.2 19.8 copy-start.31
  415.2 37.5 %copy-start.29 = (bf16[32,32]{1,0:T(8,128)(2,1)S(1)}, bf16[32,32]{1,0:T(8,128)(2,1)}, u32[]{:S(2)}) copy-start(bf16[32,32]{1,0:T(8,128)(2,1)} %param.25) | copy-start | bytes 6148
  415.2 350.1 %all-gather.21.cloned.1.call-start = ((), (), s32[]{:S(2)}) async-start(), calls=%async_computation.10 | async-start | bytes 20971520 | tf_op jit(solution)/shard_map/all_gather | solution.py:133
  416.0 635.9 %all-gather.23.cloned.1.call-start = ((), (), s32[]{:S(2)}) async-start(), calls=%async_computation.11 | async-start | bytes 20971520 | tf_op jit(solution)/shard_map/all_gather | solution.py:134
  416.7 714.1 %all-reduce.10.cloned.1.call-start = ((), (), s32[]{:S(2)}) async-start(), calls=%async_computation.12 | async-start | bytes 4194304 | tf_op jit(solution)/shard_map/psum | solution.py:140
  466.2 664.7 %copy-start.24 = (f32[2048]{0:T(1024)}, f32[2048]{0:T(1024)S(1)}, u32[]{:S(2)}) copy-start(f32[2048]{0:T(1024)S(1)} %get-tuple-element.164) | copy-start | bytes 24580
  1069.5 172.7 %all-reduce.12.cloned.1.call-start = ((), (), s32[]{:S(2)}) async-start(), calls=%async_computation.13 | async-start | bytes 4194304 | tf_op jit(solution)/shard_map/psum | solution.py:157
  1143.2 20.5 copy-start.6
  1179.1 263.4 %reduce-scatter.4.cloned.1.call-start = ((), (), s32[]{:S(2)}) async-start(), calls=%async_computation.14 | async-start | bytes 5242880 | tf_op jit(solution)/shard_map/reduce_scatter | solution.py:167
  1397.9 91.5 %reduce-scatter.6.cloned.1.call-start = ((), (), s32[]{:S(2)}) async-start(), calls=%async_computation.15 | async-start | bytes 5242880 | tf_op jit(solution)/shard_map/reduce_scatter | solution.py:170
  1398.6 966.6 %reduce-scatter.8.cloned.1.call-start = ((), (), s32[]{:S(2)}) async-start(), calls=%async_computation.17 | async-start | bytes 62914560 | tf_op jit(solution)/shard_map/reduce_scatter | solution.py:203
  1512.5 15.4 copy-start.8
  1544.3 916.1 %all-reduce.18.cloned.1.call-start = ((), (), s32[]{:S(2)}) async-start(), calls=%async_computation.19 | async-start | bytes 148480 | tf_op jit(solution)/shard_map/psum | solution.py:200
  1558.4 968.9 %all-reduce.14.cloned.1.call-start = ((), (), s32[]{:S(2)}) async-start(), calls=%async_computation.16 | async-start | bytes 4194304 | tf_op jit(solution)/shard_map/psum | solution.py:181
  1567.3 1183.0 %all-reduce.16.cloned.1.call-start = ((), (), s32[]{:S(2)}) async-start(), calls=%async_computation.18 | async-start | bytes 25165824 | tf_op jit(solution)/shard_map/psum | solution.py:219
  (57 other events, 189.7 us)
Sparse Core Ops, SparseCore 0:
  9.6 83.4 all-gather.10
  94.6 79.7 all-gather.14
  176.0 79.2 all-gather.8
  257.3 32.9 all-gather.12
  292.2 34.4 all-gather.16
  328.1 80.7 all-gather.18
  415.3 61.6 all-reduce.7
  478.5 286.7 all-gather.20
  766.9 284.9 all-gather.22
  1069.6 61.1 all-reduce.9
  1179.2 62.9 all-reduce.11
  1398.0 44.3 reduce-scatter.3
  1445.0 44.3 reduce-scatter.5
  1544.4 820.7 reduce-scatter.7
  2370.3 90.0 all-reduce.17
  2463.1 64.0 all-reduce.13
  2529.6 220.6 all-reduce.15
where the time goes:
time: 2780 us; the launch traced here: 2770 us
  waiting for transfers between devices  2230 us (80%)
  matrix products  297 us (11%)
  local copies, waits for them, and re-layouts  124 us (4%)
  blocking collectives  62.7 us (2%)
  other arithmetic  46.4 us (2%)
    reduce_scatter x1, waiting for transfers between devices, shards(): lax.psum_scatter(jnp.concatenate([transposed_times(tokens, grad_queries),...  798 us
    all_gather x1, waiting for transfers between devices, shards(): lax.all_gather(up_weight, 'shard', axis=0, tiled=True)  285 us
    all_gather x1, waiting for transfers between devices, shards(): lax.all_gather(down_weight, 'shard', axis=0, tiled=True)  271 us
    psum x1, waiting for transfers between devices, shards(): summed = lax.psum(summed.astype(jnp.bfloat16), 'ctx').astype(jnp.float32)  218 us
    dot_general x30, matrix products, times_transposed(): lax.dot_general(left, right, (((1,), (1,)), ((), ())), preferred_element_...  104 us
    dot_general x22, matrix products, transposed_times(): lax.dot_general(left, right, (((0,), (0,)), ((), ())), preferred_element_...  101 us
    psum x1, waiting for transfers between devices, shards(): lax.psum((qv_sums, up_sums, gain_sums, bias_sums, square_sums), ('shard',...  95.1 us
    dot_general x22, matrix products, product(): return jnp.dot(left, right, preferred_element_type=jnp.float32)  91.5 us
  transfers between devices with their start and end apart: 17, of which 17 were waited for; matrix products, arithmetic and copies ran while one was open for 6% of the time, Pallas kernels for 0%

commit v1 on v0

--- a/solution.py
+++ b/solution.py
@@ -1,3 +1,4 @@
+import functools
 import jax
 import jax.numpy as jnp
 from jax import lax
@@ -7,6 +8,27 @@
 H = 16
 DH = 128
 epsilon = 1e-12
+
+
+def store_tails(arr_in, row_axis):
+    how_many = lax.axis_size(row_axis)
+    v_now = range(how_many)
+    local_part = map(lambda w: (w, (w + 1) % how_many), v_now)
+    fields = list(local_part)
+    z = map(lambda w: (w, (w - 1) % how_many), range(how_many))
+    panels = list(z)
+    d_next, now = ([arr_in], [arr_in])
+    for _ in range(how_many // 2):
+        item_now = lax.ppermute(d_next[-1], axis_name=row_axis, perm=fields)
+        d_next.append(item_now)
+    for _ in [*range((how_many - 1) // 2)]:
+        last = lax.ppermute(now[-1], row_axis, perm=panels)
+        now.append(last)
+    aux = jnp.concatenate([*d_next[::-1], *now[1:]], 0)
+    return jnp.roll(aux, (lax.axis_index(row_axis) - how_many // 2) * arr_in.shape[0], 0)
+
+
+answer_bands = functools.partial(store_tails, row_axis="shard")
 
 
 def product(left, right):
@@ -96,7 +118,7 @@
     gathered = (
         lax.all_gather(query_weight, "shard", axis=0, tiled=True),
         lax.all_gather(key_weight, "shard", axis=0, tiled=True),
-        lax.all_gather(value_weight, "shard", axis=0, tiled=True),
+        answer_bands(value_weight),
         lax.all_gather(output_weight, "shard", axis=0, tiled=True),
         lax.all_gather(query_value_bias, "shard", axis=2, tiled=True),
         lax.all_gather(norm_gains, "shard", axis=2, tiled=True),

time: 2780 us -> 2760 us (level)
  waiting for transfers between devices: 2230 us -> 2100 us
  blocking collectives: 62.7 us -> 138 us
    all_gather x1, waiting for transfers between devices: 83.6 us -> 0.02 us  [shards(): lax.all_gather(key_weight, 'shard', axis=0, tiled=True)]
    all_gather x1, blocking collectives: 13.9 us -> 88.8 us  [shards(): lax.all_gather(query_value_bias, 'shard', axis=2, tiled=True)]
    all_gather x1 -> x0, waiting for transfers between devices: 61.1 us -> none  [shards(): lax.all_gather(value_weight, 'shard', axis=0, tiled=True)]
    ppermute x0 -> x3, waiting for transfers between devices: none -> 38.4 us  [the longest x2 38.4 us: store_tails(): item_now = lax.ppermute(d_next[-1], axis_name=row_axis, perm=fields)]
  transfers between devices with their start and end apart: 17 -> 19, of which waited for: 17 -> 16; matrix products, arithmetic and copies ran while one was open for 6% -> 6% of each run, Pallas kernels for 0% -> 0%
where the time goes in v1:
time: 2760 us; the launch traced here: 2750 us
  waiting for transfers between devices  2100 us (76%)
  matrix products  296 us (11%)
  blocking collectives  138 us (5%)
  local copies, waits for them, and re-layouts  135 us (5%)
  other arithmetic  46.3 us (2%)
    reduce_scatter x1, waiting for transfers between devices, shards(): lax.psum_scatter(jnp.concatenate([transposed_times(tokens, grad_queries),...  796 us
    all_gather x1, waiting for transfers between devices, shards(): lax.all_gather(up_weight, 'shard', axis=0, tiled=True)  285 us
    all_gather x1, waiting for transfers between devices, shards(): lax.all_gather(down_weight, 'shard', axis=0, tiled=True)  271 us
    psum x1, waiting for transfers between devices, shards(): summed = lax.psum(summed.astype(jnp.bfloat16), 'ctx').astype(jnp.float32)  218 us
    dot_general x30, matrix products, times_transposed(): lax.dot_general(left, right, (((1,), (1,)), ((), ())), preferred_element_...  106 us
    dot_general x22, matrix products, transposed_times(): lax.dot_general(left, right, (((0,), (0,)), ((), ())), preferred_element_...  101 us
    psum x1, waiting for transfers between devices, shards(): lax.psum((qv_sums, up_sums, gain_sums, bias_sums, square_sums), ('shard',...  95.2 us
    all_gather x1, blocking collectives, shards(): lax.all_gather(query_value_bias, 'shard', axis=2, tiled=True)  88.8 us
  transfers between devices with their start and end apart: 19, of which 16 were waited for; matrix products, arithmetic and copies ran while one was open for 6% of the time, Pallas kernels for 0%

profile of v1, /device:TPU:0, one launch (start us, length us, event | category | flops | bytes accessed | tf_op | source)
XLA Modules:
  0.0 2748.2 jit_solution(9740927569005020771)
XLA Ops:
  11.8 38.4 %collective-permute-done = bf16[512,1024]{1,0:T(8,128)(2,1)S(1)} collective-permute-done((bf16[512,1024]{1,0:T(8,128)(2,1)}, bf16[512,1024]{1,0:T(8,128)(2,1)S(1)}, u32[]{:S(2)}, u32[]{:S(2)}) %collective-permute-start) | collective-permute-done | bytes 1048608 | tf_op jit(solution)/shard_map/ppermute | solution.py:22
  50.2 15.0 collective-permute-start.1
  68.5 88.8 %all_gather.40 = bf16[2,8,128]{1,0,2:T(2,128)(2,1)S(1)} all-gather(bf16[2,8,32]{1,0,2:T(2,128)(2,1)S(1)} %copy.61), channel_id=1, replica_groups=mesh['shard'=4,'ctx'=4,'tp'=2] {'shard'}, dimensions={2}, use_global_device_ids=true | all-gather | bytes 5120 | tf_op jit(solution)/shard_map/all_gather | solution.py:123
  176.5 52.5 %all-gather.8.cloned.1.call-done = bf16[2048,1024]{1,0:T(8,128)(2,1)} async-done(((bf16[512,1024]{1,0:T(8,128)(2,1)}), bf16[2048,1024]{1,0:T(8,128)(2,1)}) %all-gather.8.cloned.1.call-update) | async-done | bytes 4194320 | tf_op jit(solution)/shard_map/all_gather | solution.py:119
  233.8 30.4 %all-gather.14.cloned.1.call-done = bf16[2048,1024]{0,1:T(8,128)(2,1)} async-done(((bf16[512,1024]{0,1:T(8,128)(2,1)}), bf16[2048,1024]{0,1:T(8,128)(2,1)}) %all-gather.14.cloned.1.call-update) | async-done | bytes 4194320 | tf_op jit(solution)/shard_map/all_gather | solution.py:142
  270.6 30.1 %all-gather.12.cloned.1.call-done = bf16[2048,1024]{1,0:T(8,128)(2,1)} async-done(((bf16[512,1024]{1,0:T(8,128)(2,1)}), bf16[2048,1024]{1,0:T(8,128)(2,1)}) %all-gather.12.cloned.1.call-update) | async-done | bytes 4194320 | tf_op jit(solution)/shard_map/all_gather | solution.py:141
  306.7 44.9 %while.26 = (s32[]{:T(128)}, bf16[8,512,128]{1,2,0:T(8,128)(2,1)}, f32[8,512]{1,0:T(8,128)S(1)}, bf16[8,512,128]{2,1,0:T(8,128)(2,1)S(1)}, bf16[8,2048,128]{2,1,...) while((s32[]{:T(128)}, bf16[8,512,128]{1,2,0:T(8,128)(2,1)}, ...), condition=%wide.region_3.4_spmd, body=%wide.region_0.3_spmd.sunk | while | flops 546307584 | bytes 14047329 | solution.py:147
  351.6 31.2 %all-gather.16.cloned.1.call-done = bf16[2048,1024]{1,0:T(8,128)(2,1)} async-done(((bf16[512,1024]{1,0:T(8,128)(2,1)}), bf16[2048,1024]{1,0:T(8,128)(2,1)}) %all-gather.16.cloned.1.call-update) | async-done | bytes 4194320 | tf_op jit(solution)/shard_map/all_gather | solution.py:122
  454.5 284.8 %all-gather.18.cloned.1.call-done = bf16[2048,4096]{1,0:T(8,128)(2,1)} async-done(((bf16[512,4096]{1,0:T(8,128)(2,1)}), bf16[2048,4096]{1,0:T(8,128)(2,1)}) %all-gather.18.cloned.1.call-update) | async-done | bytes 16777232 | tf_op jit(solution)/shard_map/all_gather | solution.py:155
  739.3 15.4 fusion.93
  754.6 271.2 %all-gather.20.cloned.1.call-done = bf16[2048,4096]{1,0:T(8,128)(2,1)} async-done(((bf16[512,4096]{1,0:T(8,128)(2,1)}), bf16[2048,4096]{1,0:T(8,128)(2,1)}) %all-gather.20.cloned.1.call-update) | async-done | bytes 16777232 | tf_op jit(solution)/shard_map/all_gather | solution.py:156
  1025.8 17.6 convolution_convert_fusion.3
  1043.7 61.1 %all-reduce.10.cloned.1.call-done = bf16[512,2048]{1,0:T(8,128)(2,1)} async-done(((bf16[512,2048]{1,0:T(8,128)(2,1)}), bf16[512,2048]{1,0:T(8,128)(2,1)}) %all-reduce.10.cloned.1.call-update) | async-done | bytes 2097168 | tf_op jit(solution)/shard_map/psum | solution.py:162
  1117.1 20.5 convert_reduce_fusion
  1153.1 63.1 %all-reduce.12.cloned.1.call-done = bf16[512,2048]{1,0:T(8,128)(2,1)} async-done(((bf16[512,2048]{1,0:T(8,128)(2,1)}), bf16[512,2048]{1,0:T(8,128)(2,1)}) %all-reduce.12.cloned.1.call-update) | async-done | bytes 2097168 | tf_op jit(solution)/shard_map/psum | solution.py:179
  1232.7 138.9 %while.27 = (s32[]{:T(128)}, bf16[8,512,128]{1,2,0:T(8,128)(2,1)}, bf16[8,2048,128]{1,2,0:T(8,128)(2,1)}, bf16[8,2048,128]{1,2,0:T(8,128)(2,1)}, bf16[8,512,128]...) while((s32[]{:T(128)}, bf16[8,512,128]{1,2,0:T(8,128)(2,1)}, ...), condition=%wide.region_17.18_spmd, body=%wide.region_15.17_spmd.sunk | while | flops 1351220736 | bytes 71447792 | solution.py:184
  1401.7 14.5 reduce-scatter.4.cloned.1.call-done
  1428.5 34.6 %reduce-scatter.6.cloned.1.call-done = bf16[512,1024]{0,1:T(8,128)(2,1)} async-done(((bf16[2048,1024]{0,1:T(8,128)(2,1)}), bf16[512,1024]{0,1:T(8,128)(2,1)}) %reduce-scatter.6.cloned.1.call-update) | async-done | bytes 1048592 | tf_op jit(solution)/shard_map/reduce_scatter | solution.py:192
  1486.2 15.3 convert_dynamic-update-slice_fusion.1
  1501.4 16.2 convert_dynamic-update-slice_fusion
  1543.0 795.7 %reduce-scatter.8.cloned.1.call-done = bf16[512,12288]{1,0:T(8,128)(2,1)} async-done(((bf16[2048,12288]{1,0:T(8,128)(2,1)}), bf16[512,12288]{1,0:T(8,128)(2,1)}) %reduce-scatter.8.cloned.1.call-update) | async-done | bytes 12582928 | tf_op jit(solution)/shard_map/reduce_scatter | solution.py:225
  2338.7 95.2 %all-reduce.18.cloned.1.call-done = (f32[2,8,128]{2,1,0:T(8,128)}, f32[32,128]{1,0:T(8,128)}, f32[2,16,128]{2,1,0:T(8,128)}, f32[4,16,128]{2,1,0:T(8,128)}, f32[3]{0:T(128)}) async-done(((f32[2,8,128]{2,1,0:T(8,128)}, f32[32,128]{1,0:T(8,128)}, f32[2,16,128]{2,1,0:T(8,128)}, f32[4,16,128]{2,1,0:T(8,128)}, f32[3]{0:T(128)}), (f32[2,8,128]{2,1,0:T(8,128)}, f32[32,128]{1,0:T(8,128)}, f32[2,16,128]{2,1,0:T(8,128)}, ...) | async-done | bytes 73756 | tf_op jit(solution)/shard_map/psum | solution.py:222
  2440.6 60.1 %all-reduce.14.cloned.1.call-done = bf16[512,2048]{1,0:T(8,128)(2,1)} async-done(((bf16[512,2048]{1,0:T(8,128)(2,1)}), bf16[512,2048]{1,0:T(8,128)(2,1)}) %all-reduce.14.cloned.1.call-update) | async-done | bytes 2097168 | tf_op jit(solution)/shard_map/psum | solution.py:203
  2505.6 218.1 %all-reduce.16.cloned.1.call-done = bf16[512,12288]{1,0:T(8,128)(2,1)} async-done(((bf16[512,12288]{1,0:T(8,128)(2,1)}), bf16[512,12288]{1,0:T(8,128)(2,1)}) %all-reduce.16.cloned.1.call-update) | async-done | bytes 12582928 | tf_op jit(solution)/shard_map/psum | solution.py:241
  (385 shorter events, 463.4 us)
Async XLA Ops:
  7.2 151.7 %copy-start.16 = (bf16[512,1024]{1,0:T(8,128)(2,1)S(1)}, bf16[512,1024]{1,0:T(8,128)(2,1)}, u32[]{:S(2)}) copy-start(bf16[512,1024]{1,0:T(8,128)(2,1)} %param.20) | copy-start | bytes 3145732
  7.2 162.6 %all-gather.10.cloned.1.call-start = ((), (), s32[]{:S(2)}) async-start(), calls=%async_computation.4 | async-start | bytes 5242880 | tf_op jit(solution)/shard_map/all_gather | solution.py:120
  7.9 221.1 %all-gather.8.cloned.1.call-start = ((), (), s32[]{:S(2)}) async-start(), calls=%async_computation.3 | async-start | bytes 5242880 | tf_op jit(solution)/shard_map/all_gather | solution.py:119
  8.7 255.5 %all-gather.14.cloned.1.call-start = ((), (), s32[]{:S(2)}) async-start(), calls=%async_computation.6 | async-start | bytes 5242880 | tf_op jit(solution)/shard_map/all_gather | solution.py:142
  8.7 41.5 %collective-permute-start = (bf16[512,1024]{1,0:T(8,128)(2,1)}, bf16[512,1024]{1,0:T(8,128)(2,1)S(1)}, u32[]{:S(2)}, u32[]{:S(2)}) collective-permute-start(bf16[512,1024]{1,0:T(8,128)(2,1)} %param.20), channel_id=1, source_target_pairs={{0,8},{8,16},{16,24},{24,0},{1,9},{9,17},{17,25},{25,1},{2,10},{10... | collective-permute-start | bytes 3145736 | tf_op jit(solution)/shard_map/ppermute | solution.py:22
  50.2 108.8 %copy-start.17 = (bf16[512,1024]{1,0:T(8,128)(2,1)}, bf16[512,1024]{1,0:T(8,128)(2,1)S(1)}, u32[]{:S(2)}) copy-start(bf16[512,1024]{1,0:T(8,128)(2,1)S(1)} %collective-permute-done) | copy-start | bytes 3145732
  50.2 107.2 %collective-permute-start.1 = (bf16[512,1024]{1,0:T(8,128)(2,1)S(1)}, bf16[512,1024]{1,0:T(8,128)(2,1)}, u32[]{:S(2)}, u32[]{:S(2)}) collective-permute-start(bf16[512,1024]{1,0:T(8,128)(2,1)S(1)} %collective-permute-done), channel_id=1, source_target_pairs={{0,8},{8,16},{16,24},{24,0},{1,9},{9,17},{17,25},{25,1},{2,10},{10... | collective-permute-start | bytes 3145736 | tf_op jit(solution)/shard_map/ppermute | solution.py:22
  65.2 93.8 %collective-permute-start.2 = (bf16[512,1024]{1,0:T(8,128)(2,1)}, bf16[512,1024]{1,0:T(8,128)(2,1)S(1)}, u32[]{:S(2)}, u32[]{:S(2)}) collective-permute-start(bf16[512,1024]{1,0:T(8,128)(2,1)} %param.20), channel_id=1, source_target_pairs={{0,24},{8,0},{16,8},{24,16},{1,25},{9,1},{17,9},{25,17},{2,26},{10... | collective-permute-start | bytes 3145736 | tf_op jit(solution)/shard_map/ppermute | solution.py:25
  169.8 130.9 %all-gather.12.cloned.1.call-start = ((), (), s32[]{:S(2)}) async-start(), calls=%async_computation.5 | async-start | bytes 5242880 | tf_op jit(solution)/shard_map/all_gather | solution.py:141
  175.4 207.5 %all-gather.16.cloned.1.call-start = ((), (), s32[]{:S(2)}) async-start(), calls=%async_computation.7 | async-start | bytes 5242880 | tf_op jit(solution)/shard_map/all_gather | solution.py:122
  176.0 274.9 %all-reduce.8.cloned.1.call-start = ((), (), s32[]{:S(2)}) async-start(), calls=%async_computation.8 | async-start | bytes 4194304 | tf_op jit(solution)/shard_map/psum | solution.py:150
  389.1 37.5 %copy-start.31 = (bf16[32,32]{1,0:T(8,128)(2,1)S(1)}, bf16[32,32]{1,0:T(8,128)(2,1)}, u32[]{:S(2)}) copy-start(bf16[32,32]{1,0:T(8,128)(2,1)} %param.25) | copy-start | bytes 6148
  389.1 350.1 %all-gather.18.cloned.1.call-start = ((), (), s32[]{:S(2)}) async-start(), calls=%async_computation.9 | async-start | bytes 20971520 | tf_op jit(solution)/shard_map/all_gather | solution.py:155
  389.9 635.9 %all-gather.20.cloned.1.call-start = ((), (), s32[]{:S(2)}) async-start(), calls=%async_computation.10 | async-start | bytes 20971520 | tf_op jit(solution)/shard_map/all_gather | solution.py:156
  390.6 714.1 %all-reduce.10.cloned.1.call-start = ((), (), s32[]{:S(2)}) async-start(), calls=%async_computation.11 | async-start | bytes 4194304 | tf_op jit(solution)/shard_map/psum | solution.py:162
  440.1 664.7 %copy-start.26 = (f32[2048]{0:T(1024)}, f32[2048]{0:T(1024)S(1)}, u32[]{:S(2)}) copy-start(f32[2048]{0:T(1024)S(1)} %get-tuple-element.164) | copy-start | bytes 24580
  1043.4 172.7 %all-reduce.12.cloned.1.call-start = ((), (), s32[]{:S(2)}) async-start(), calls=%async_computation.12 | async-start | bytes 4194304 | tf_op jit(solution)/shard_map/psum | solution.py:179
  1117.1 20.5 copy-start.6
  1153.0 263.2 %reduce-scatter.4.cloned.1.call-start = ((), (), s32[]{:S(2)}) async-start(), calls=%async_computation.13 | async-start | bytes 5242880 | tf_op jit(solution)/shard_map/reduce_scatter | solution.py:189
  1371.7 91.4 %reduce-scatter.6.cloned.1.call-start = ((), (), s32[]{:S(2)}) async-start(), calls=%async_computation.14 | async-start | bytes 5242880 | tf_op jit(solution)/shard_map/reduce_scatter | solution.py:192
  1372.3 966.4 %reduce-scatter.8.cloned.1.call-start = ((), (), s32[]{:S(2)}) async-start(), calls=%async_computation.16 | async-start | bytes 62914560 | tf_op jit(solution)/shard_map/reduce_scatter | solution.py:225
  1517.7 916.1 %all-reduce.18.cloned.1.call-start = ((), (), s32[]{:S(2)}) async-start(), calls=%async_computation.18 | async-start | bytes 148480 | tf_op jit(solution)/shard_map/psum | solution.py:222
  1531.9 968.8 %all-reduce.14.cloned.1.call-start = ((), (), s32[]{:S(2)}) async-start(), calls=%async_computation.15 | async-start | bytes 4194304 | tf_op jit(solution)/shard_map/psum | solution.py:203
  1542.9 1180.8 %all-reduce.16.cloned.1.call-start = ((), (), s32[]{:S(2)}) async-start(), calls=%async_computation.17 | async-start | bytes 25165824 | tf_op jit(solution)/shard_map/psum | solution.py:241
  (59 other events, 205.0 us)
Sparse Core Ops, SparseCore 0:
  9.6 138.9 all-gather.9
  150.1 78.9 all-gather.7
  231.2 32.9 all-gather.13
  266.1 34.4 all-gather.11
  302.1 80.7 all-gather.15
  389.2 61.6 all-reduce.7
  452.5 286.7 all-gather.17
  740.8 284.9 all-gather.19
  1043.5 61.1 all-reduce.9
  1153.1 62.9 all-reduce.11
  1371.8 44.3 reduce-scatter.3
  1418.6 44.3 reduce-scatter.5
  1517.8 820.7 reduce-scatter.7
  2343.8 90.0 all-reduce.17
  2436.6 64.0 all-reduce.13
  2503.0 220.6 all-reduce.15
